TPU v7x, 128 devices: a whole 4x4x4 slice. The times are simulated.
128 devices in a mesh: row: 4 (over z), col: 16 (over x, y), gz: 2 (over core).
Axes of the slice: x: 4, y: 4, z: 4, core: 2. Of those that a mesh axis runs over, the one named last changes fastest.
Arguments:
- rhs_half: float32 [2, 3, 64, 4096], P('gz', None, None, ('row', 'col')), may hold values from -6 to 6
- rhs_root: float32 [64, 4096], P(None, ('row', 'col')), may hold values from -6 to 6
- lower_coupling: bfloat16 [2, 5, 4096, 4096], P('gz', None, 'col', 'row'), may hold values from -0.046875 to 0.046875
- lower_pattern: int32 [2, 5, 32, 32], P('gz', None, 'col', 'row'), may hold values 0 or 1
- upper_coupling: bfloat16 [2, 5, 4096, 4096], P('gz', None, 'col', 'row'), may hold values from -0.046875 to 0.046875
- upper_pattern: int32 [2, 5, 32, 32], P('gz', None, 'col', 'row'), may hold values 0 or 1
- lower_inverse: bfloat16 [2, 3, 4096, 4096], P('gz', None, 'col', 'row'), may hold values from -0.09375 to 0.09375
- upper_inverse: bfloat16 [2, 3, 4096, 4096], P('gz', None, 'col', 'row'), may hold values from -0.09375 to 0.09375
- root_lower_inverse: bfloat16 [4096, 4096], P('col', 'row'), may hold values from -0.09375 to 0.09375
- root_upper_inverse: bfloat16 [4096, 4096], P('col', 'row'), may hold values from -0.09375 to 0.09375
Outputs:
- sol_half: float32 [2, 3, 64, 4096], P('gz', None, None, ('row', 'col'))
- sol_root: float32 [64, 4096], P(None, ('row', 'col'))
All inputs are finite; a program needn't handle non-finite values. No bound on the sum of `lower_pattern` or of `upper_pattern` on one device may be relied on, other than what follows from the above.
Results may differ from a plain program's by a relative error of at most 0.007.
Values may be sent and summed in bfloat16 or wider, within the bound.
A program may use at most 64 MiB of HBM per device.

v0:
```python
import jax
import jax.numpy as jnp
from jax import lax
from jax.sharding import PartitionSpec as P


def apply_mask(tiles, pattern):
    count, across, down = pattern.shape
    shaped = tiles.reshape(count, across, tiles.shape[1] // across, down, tiles.shape[2] // down)
    shaped = shaped * pattern[:, :, None, :, None].astype(jnp.bfloat16)
    return shaped.reshape(tiles.shape)


def multiply(vectors, tiles):
    return jnp.einsum("snj,sji->sni", vectors, tiles, preferred_element_type=jnp.float32)


def multiply_one(vectors, tiles):
    return jnp.einsum("nj,sji->sni", vectors[0], tiles, preferred_element_type=jnp.float32)


def settle(partial_value, offset_bias, column, narrow):
    share_width = offset_bias.shape[2]
    slot = (
        lax.dynamic_slice_in_dim(partial_value, column * share_width, share_width, 2) + offset_bias
    )
    partial_value = lax.dynamic_update_slice_in_dim(partial_value, slot, column * share_width, 2)
    summed = lax.psum(partial_value, "col")
    owned = lax.dynamic_slice_in_dim(summed, column * share_width, share_width, 2)
    gathered = lax.all_gather(summed.astype(jnp.bfloat16), "row", axis=2, tiled=True)
    return (owned, lax.dynamic_slice_in_dim(gathered, column * narrow, narrow, 2))


def per_device(
    rhs_half,
    rhs_root,
    lower_coupling,
    lower_pattern,
    upper_coupling,
    upper_pattern,
    lower_inverse,
    upper_inverse,
    root_lower_inverse,
    root_upper_inverse,
):
    column = lax.axis_index("col")
    lower = apply_mask(lower_coupling[0], lower_pattern[0])
    upper = apply_mask(upper_coupling[0], upper_pattern[0])
    narrow = lower.shape[1]
    share_width = rhs_half.shape[3]
    nrhs_count = rhs_half.shape[2]

    def zeros_for(count):
        return jnp.zeros((count, nrhs_count, share_width), jnp.float32)

    leaf_full = lax.all_gather(
        rhs_half[0, 1:3].astype(jnp.bfloat16), ("row", "col"), axis=2, tiled=True
    )
    leaf_input = lax.dynamic_slice_in_dim(leaf_full, column * narrow, narrow, 2)
    leaf_value, leaf_cols = settle(
        multiply(leaf_input, lower_inverse[0, 1:3]), zeros_for(2), column, narrow
    )
    top_terms = -multiply(leaf_cols, lower[0:2]).sum(axis=0, keepdims=True)
    top_rest, top_input = settle(top_terms, rhs_half[0, 0:1], column, narrow)
    top_value, top_cols = settle(
        multiply(top_input, lower_inverse[0, 0:1]), zeros_for(1), column, narrow
    )
    every_cols = jnp.concatenate([top_cols, leaf_cols], axis=0)
    root_terms = -multiply(every_cols, lower[2:5]).sum(axis=0, keepdims=True)
    root_terms = lax.psum(root_terms, "gz")
    root_rest, root_input = settle(root_terms, rhs_root[None], column, narrow)
    root_value, root_cols = settle(
        multiply(root_input, root_lower_inverse[None]), zeros_for(1), column, narrow
    )
    root_back, root_back_cols = settle(
        multiply(root_cols, root_upper_inverse[None]), zeros_for(1), column, narrow
    )
    first_terms = -multiply_one(root_back_cols, upper[2:3])
    first_rest, first_input = settle(first_terms, top_value, column, narrow)
    first_back, first_back_cols = settle(
        multiply(first_input, upper_inverse[0, 0:1]), zeros_for(1), column, narrow
    )
    second_terms = -(
        multiply_one(root_back_cols, upper[3:5]) + multiply_one(first_back_cols, upper[0:2])
    )
    second_rest, second_input = settle(second_terms, leaf_value, column, narrow)
    second_back, second_back_cols = settle(
        multiply(second_input, upper_inverse[0, 1:3]), zeros_for(2), column, narrow
    )
    sol_half = jnp.concatenate([first_back, second_back], axis=0)[None]
    return (sol_half, root_back[0])


def solution(mesh):
    in_specs = (
        P("gz", None, None, ("row", "col")),
        P(None, ("row", "col")),
        P("gz", None, "col", "row"),
        P("gz", None, "col", "row"),
        P("gz", None, "col", "row"),
        P("gz", None, "col", "row"),
        P("gz", None, "col", "row"),
        P("gz", None, "col", "row"),
        P("col", "row"),
        P("col", "row"),
    )
    out_specs = (P("gz", None, None, ("row", "col")), P(None, ("row", "col")))
    return jax.shard_map(
        per_device, mesh=mesh, in_specs=in_specs, out_specs=out_specs, check_vma=False
    )
```

profile of v0, /device:TPU:0, one launch (start us, length us, event | category | flops | bytes accessed | tf_op | source)
XLA Modules:
  0.0 1071.1 jit_solution(17997548227670011957)
XLA Ops:
  9.0 70.3 %all-gather.9.cloned.1.call-done = bf16[1,2,64,4096]{2,1,0,3:T(2,128)(2,1)} async-done(((bf16[1,2,64,64]{2,1,0,3:T(2,128)(2,1)}), bf16[1,2,64,4096]{2,1,0,3:T(2,128)(2,1)}) %all-gather.9.cloned.1.call-update) | async-done | bytes 1048592 | tf_op jit(solution)/shard_map/all_gather | solution.py:56
  84.5 83.1 %all-reduce.12.cloned.1.call-done = f32[2,64,1024]{2,1,0:T(8,128)} async-done(((f32[2,64,1024]{2,1,0:T(8,128)}), f32[2,64,1024]{2,1,0:T(8,128)}) %all-reduce.12.cloned.1.call-update) | async-done | bytes 524304 | tf_op jit(solution)/shard_map/psum | solution.py:28
  171.4 2.3 slice.51
  173.7 19.6 %all-gather.5.cloned.1.call-done = bf16[2,64,4096]{2,1,0:T(8,128)(2,1)} async-done(((bf16[2,64,1024]{2,1,0:T(8,128)(2,1)}), bf16[2,64,4096]{2,1,0:T(8,128)(2,1)}) %all-gather.5.cloned.1.call-update) | async-done | bytes 1048592 | tf_op jit(solution)/shard_map/all_gather | solution.py:30
  197.0 77.2 %all-reduce.23 = bf16[1,64,1024]{2,1,0:T(8,128)(2,1)} all-reduce(f32[1,64,1024]{2,1,0:T(8,128)S(1)} %dynamic_update_slice.31), channel_id=1, replica_groups=mesh['row'=4,'col'=16,'gz'=2] {'col'}, use_global_device_ids=true, to_apply=%region_1.0 | all-reduce | flops 65536 | bytes 393216 | tf_op jit(solution)/shard_map/psum | solution.py:28
  274.2 13.0 %all_gather.32 = bf16[1,64,4096]{2,1,0:T(8,128)(2,1)S(1)} all-gather(bf16[1,64,1024]{2,1,0:T(8,128)(2,1)} %all-reduce.23), channel_id=1, replica_groups=mesh['row'=4,'col'=16,'gz'=2] {'row'}, dimensions={2}, use_global_device_ids=true | all-gather | bytes 655360 | tf_op jit(solution)/shard_map/all_gather | solution.py:30
  291.0 2.5 slice.55
  293.5 3.9 copy.17
  297.4 72.5 %all-reduce.14.cloned.1.call-done = f32[1,64,1024]{2,1,0:T(8,128)} async-done(((f32[1,64,1024]{2,1,0:T(8,128)}), f32[1,64,1024]{2,1,0:T(8,128)}) %all-reduce.14.cloned.1.call-update) | async-done | bytes 262160 | tf_op jit(solution)/shard_map/psum | solution.py:28
  370.9 13.8 %all_gather.33 = bf16[1,64,4096]{2,1,0:T(8,128)(2,1)S(1)} all-gather(bf16[1,64,1024]{2,1,0:T(8,128)(2,1)S(1)} %convert_element_type.60), channel_id=1, replica_groups=mesh['row'=4,'col'=16,'gz'=2] {'row'}, dimensions={2}, use_global_device_ids=true | all-gather | bytes 655360 | tf_op jit(solution)/shard_map/all_gather | solution.py:30
  388.0 20.1 %all-reduce.16.cloned.1.call-done = f32[1,64,1024]{2,1,0:T(8,128)} async-done(((f32[1,64,1024]{2,1,0:T(8,128)}), f32[1,64,1024]{2,1,0:T(8,128)}) %all-reduce.16.cloned.1.call-update) | async-done | bytes 262160 | tf_op jit(solution)/shard_map/psum | solution.py:70
  410.4 77.5 %all-reduce.24 = bf16[1,64,1024]{2,1,0:T(8,128)(2,1)S(1)} all-reduce(f32[1,64,1024]{2,1,0:T(8,128)} %dynamic_update_slice.33), channel_id=1, replica_groups=mesh['row'=4,'col'=16,'gz'=2] {'col'}, use_global_device_ids=true, to_apply=%region_4.0 | all-reduce | flops 65536 | bytes 393216 | tf_op jit(solution)/shard_map/psum | solution.py:28
  487.9 13.3 %all_gather.34 = bf16[1,64,4096]{2,1,0:T(8,128)(2,1)S(1)} all-gather(bf16[1,64,1024]{2,1,0:T(8,128)(2,1)S(1)} %all-reduce.24), channel_id=1, replica_groups=mesh['row'=4,'col'=16,'gz'=2] {'row'}, dimensions={2}, use_global_device_ids=true | all-gather | bytes 655360 | tf_op jit(solution)/shard_map/all_gather | solution.py:30
  501.8 71.9 %all-reduce.25 = bf16[1,64,1024]{2,1,0:T(8,128)(2,1)S(1)} all-reduce(f32[1,64,1024]{2,1,0:T(8,128)S(1)} %dynamic_update_slice.34), channel_id=1, replica_groups=mesh['row'=4,'col'=16,'gz'=2] {'col'}, use_global_device_ids=true, to_apply=%region_5.0 | all-reduce | flops 65536 | bytes 393216 | tf_op jit(solution)/shard_map/psum | solution.py:28
  573.8 12.8 %all_gather.35 = bf16[1,64,4096]{2,1,0:T(8,128)(2,1)S(1)} all-gather(bf16[1,64,1024]{2,1,0:T(8,128)(2,1)S(1)} %all-reduce.25), channel_id=1, replica_groups=mesh['row'=4,'col'=16,'gz'=2] {'row'}, dimensions={2}, use_global_device_ids=true | all-gather | bytes 655360 | tf_op jit(solution)/shard_map/all_gather | solution.py:30
  593.7 77.1 %all-reduce.18.cloned.1.call-done = f32[1,64,1024]{2,1,0:T(8,128)} async-done(((f32[1,64,1024]{2,1,0:T(8,128)}), f32[1,64,1024]{2,1,0:T(8,128)}) %all-reduce.18.cloned.1.call-update) | async-done | bytes 262160 | tf_op jit(solution)/shard_map/psum | solution.py:28
  671.8 13.8 %all_gather.36 = bf16[1,64,4096]{2,1,0:T(8,128)(2,1)S(1)} all-gather(bf16[1,64,1024]{2,1,0:T(8,128)(2,1)S(1)} %convert_element_type.63), channel_id=1, replica_groups=mesh['row'=4,'col'=16,'gz'=2] {'row'}, dimensions={2}, use_global_device_ids=true | all-gather | bytes 655360 | tf_op jit(solution)/shard_map/all_gather | solution.py:30
  687.2 74.7 %all-reduce.26 = bf16[1,64,1024]{2,1,0:T(8,128)(2,1)S(1)} all-reduce(f32[1,64,1024]{2,1,0:T(8,128)S(1)} %dynamic_update_slice.36), channel_id=1, replica_groups=mesh['row'=4,'col'=16,'gz'=2] {'col'}, use_global_device_ids=true, to_apply=%region_7.0 | all-reduce | flops 65536 | bytes 393216 | tf_op jit(solution)/shard_map/psum | solution.py:28
  761.9 12.8 %all_gather.37 = bf16[1,64,4096]{2,1,0:T(8,128)(2,1)S(1)} all-gather(bf16[1,64,1024]{2,1,0:T(8,128)(2,1)S(1)} %all-reduce.26), channel_id=1, replica_groups=mesh['row'=4,'col'=16,'gz'=2] {'row'}, dimensions={2}, use_global_device_ids=true | all-gather | bytes 655360 | tf_op jit(solution)/shard_map/all_gather | solution.py:30
  779.1 78.6 %all-reduce.20.cloned.1.call-done = f32[1,64,1024]{2,1,0:T(8,128)} async-done(((f32[1,64,1024]{2,1,0:T(8,128)}), f32[1,64,1024]{2,1,0:T(8,128)}) %all-reduce.20.cloned.1.call-update) | async-done | bytes 262160 | tf_op jit(solution)/shard_map/psum | solution.py:28
  858.7 13.8 %all_gather.38 = bf16[1,64,4096]{2,1,0:T(8,128)(2,1)S(1)} all-gather(bf16[1,64,1024]{2,1,0:T(8,128)(2,1)S(1)} %convert_element_type.65), channel_id=1, replica_groups=mesh['row'=4,'col'=16,'gz'=2] {'row'}, dimensions={2}, use_global_device_ids=true | all-gather | bytes 655360 | tf_op jit(solution)/shard_map/all_gather | solution.py:30
  875.3 78.4 %all-reduce.27 = bf16[2,64,1024]{2,1,0:T(8,128)(2,1)} all-reduce(f32[2,64,1024]{2,1,0:T(8,128)S(1)} %dynamic_update_slice.38), channel_id=1, replica_groups=mesh['row'=4,'col'=16,'gz'=2] {'col'}, use_global_device_ids=true, to_apply=%region_9.0 | all-reduce | flops 131072 | bytes 786432 | tf_op jit(solution)/shard_map/psum | solution.py:28
  953.7 20.4 %all-gather.7.cloned.1.call-done = bf16[2,64,4096]{2,1,0:T(8,128)(2,1)} async-done(((bf16[2,64,1024]{2,1,0:T(8,128)(2,1)}), bf16[2,64,4096]{2,1,0:T(8,128)(2,1)}) %all-gather.7.cloned.1.call-update) | async-done | bytes 1048592 | tf_op jit(solution)/shard_map/all_gather | solution.py:30
  979.4 83.6 %all-reduce.22.cloned.1.call-done = f32[2,64,1024]{2,1,0:T(8,128)} async-done(((f32[2,64,1024]{2,1,0:T(8,128)}), f32[2,64,1024]{2,1,0:T(8,128)}) %all-reduce.22.cloned.1.call-update) | async-done | bytes 524304 | tf_op jit(solution)/shard_map/psum | solution.py:28
  (99 shorter events, 49.7 us)
Async XLA Ops:
  7.2 494.0 %copy-start = (bf16[256,1024]{1,0:T(8,128)(2,1)S(1)}, bf16[256,1024]{1,0:T(8,128)(2,1)}, u32[]{:S(2)}) copy-start(bf16[256,1024]{1,0:T(8,128)(2,1)} %param.18) | copy-start | bytes 1572868
  7.2 162.2 %copy-start.2 = (bf16[1,5,256,1024]{3,2,1,0:T(8,128)(2,1)S(1)}, bf16[1,5,256,1024]{3,2,1,0:T(8,128)(2,1)}, u32[]{:S(2)}) copy-start(bf16[1,5,256,1024]{3,2,1,0:T(8,128)(2,1)} %param.12) | copy-start | bytes 7864324
  7.2 72.2 %all-gather.9.cloned.1.call-start = ((), (), s32[]{:S(2)}) async-start(), calls=%async_computation.8 | async-start | bytes 2129920 | tf_op jit(solution)/shard_map/all_gather | solution.py:56
  9.0 158.6 %all-reduce.12.cloned.1.call-start = ((), (), s32[]{:S(2)}) async-start(), calls=%async_computation | async-start | bytes 1048576 | tf_op jit(solution)/shard_map/psum | solution.py:28
  82.0 0.8 copy-start.3
  84.4 108.9 %all-gather.5.cloned.1.call-start = ((), (), s32[]{:S(2)}) async-start(), calls=%async_computation.1 | async-start | bytes 1310720 | tf_op jit(solution)/shard_map/all_gather | solution.py:30
  169.4 200.6 %all-reduce.14.cloned.1.call-start = ((), (), s32[]{:S(2)}) async-start(), calls=%async_computation.2 | async-start | bytes 524288 | tf_op jit(solution)/shard_map/psum | solution.py:28
  169.4 0.7 copy-start.10
  288.9 0.7 copy-start.5
  289.6 118.4 %all-reduce.16.cloned.1.call-start = ((), (), s32[]{:S(2)}) async-start(), calls=%async_computation.3 | async-start | bytes 524288 | tf_op jit(solution)/shard_map/psum | solution.py:70
  293.5 3.9 copy-start.11
  385.9 285.0 %all-reduce.18.cloned.1.call-start = ((), (), s32[]{:S(2)}) async-start(), calls=%async_computation.4 | async-start | bytes 524288 | tf_op jit(solution)/shard_map/psum | solution.py:28
  386.0 22.1 %copy-start.9 = (f32[64,64]{1,0:T(8,128)S(1)}, f32[64,64]{1,0:T(8,128)}, u32[]{:S(2)}) copy-start(f32[64,64]{1,0:T(8,128)} %param.11) | copy-start | bytes 49156
  388.0 201.2 %copy-start.1 = (bf16[5,2,128,8,128]{4,3,2,1,0:T(8,128)(2,1)}, bf16[5,2,128,8,128]{4,3,2,1,0:T(8,128)(2,1)S(1)}, u32[]{:S(2)}) copy-start(bf16[5,2,128,8,128]{4,3,2,1,0:T(8,128)(2,1)S(1)} %broadcast_multiply_fusion.1) | copy-start | bytes 7864324
  588.3 0.7 copy-start.6
  589.1 268.7 %all-reduce.20.cloned.1.call-start = ((), (), s32[]{:S(2)}) async-start(), calls=%async_computation.5 | async-start | bytes 524288 | tf_op jit(solution)/shard_map/psum | solution.py:28
  592.1 93.5 %slice-start = ((bf16[5,2,128,8,128]{4,3,2,1,0:T(8,128)(2,1)}), bf16[1,2,128,8,128]{4,3,2,1,0:T(8,128)(2,1)S(1)}, s32[]{:S(2)}) async-start(bf16[5,2,128,8,128]{4,3,2,1,0:T(8,128)(2,1)} %copy-done.1), calls=%async_computation.9 | async-start | bytes 1048576 | tf_op jit(solution)/shard_map/slice | solution.py:78
  685.7 1.1 copy-start.8
  776.5 0.7 copy-start.7
  777.2 197.0 %all-gather.7.cloned.1.call-start = ((), (), s32[]{:S(2)}) async-start(), calls=%async_computation.6 | async-start | bytes 1310720 | tf_op jit(solution)/shard_map/all_gather | solution.py:30
  953.7 109.3 %all-reduce.22.cloned.1.call-start = ((), (), s32[]{:S(2)}) async-start(), calls=%async_computation.7 | async-start | bytes 1048576 | tf_op jit(solution)/shard_map/psum | solution.py:28
  976.3 0.8 copy-start.4
Sparse Core Ops, SparseCore 0:
  11.4 67.8 all-gather.8
  84.6 82.9 all-reduce.11
  169.5 23.8 all-gather.4
  289.8 80.1 all-reduce.13
  386.0 22.0 all-reduce.15
  589.2 81.6 all-reduce.17
  777.3 80.3 all-reduce.19
  953.8 20.2 all-gather.6
  977.3 85.5 all-reduce.21
where the time goes:
time: 1070 us
  waiting for transfers between devices  526 us (49%)
  blocking collectives  473 us (44%)
  local copies, waits for them, and re-layouts  33.8 us (3%)
  between operations  14.2 us (1%)
  matrix products  13.1 us (1%)
  other arithmetic  11 us (1%)
    psum x5, waiting for transfers between devices, settle(): summed = lax.psum(partial_value, 'col')  395 us
    psum x5, blocking collectives, settle(): summed = lax.psum(partial_value, 'col')  380 us
    all_gather x7, blocking collectives, settle(): lax.all_gather(summed.astype(jnp.bfloat16), 'row', axis=2, tiled=True)  93.3 us
    all_gather x1, waiting for transfers between devices, per_device(): lax.all_gather(rhs_half[0, 1:3].astype(jnp.bfloat16), ('row', 'col'), axi...  70.3 us
    all_gather x2, waiting for transfers between devices, settle(): lax.all_gather(summed.astype(jnp.bfloat16), 'row', axis=2, tiled=True)  40 us
  transfers between devices with their start and end apart: 9, of which 9 were waited for; matrix products, arithmetic and copies ran while one was open for 2% of the time, Pallas kernels for 0%

commit v1 on v0

--- a/solution.py
+++ b/solution.py
@@ -27,7 +27,12 @@
     partial_value = lax.dynamic_update_slice_in_dim(partial_value, slot, column * share_width, 2)
     summed = lax.psum(partial_value, "col")
     owned = lax.dynamic_slice_in_dim(summed, column * share_width, share_width, 2)
-    gathered = lax.all_gather(summed.astype(jnp.bfloat16), "row", axis=2, tiled=True)
+    gathered = jnp.concatenate(
+        lax.all_to_all(
+            jnp.stack([summed.astype(jnp.bfloat16)] * lax.axis_size("row")), "row", 0, 0
+        ),
+        axis=2,
+    )
     return (owned, lax.dynamic_slice_in_dim(gathered, column * narrow, narrow, 2))
 
 

time: 1070 us -> 1040 us (0.972)
  blocking collectives: 473 us -> 434 us
  starting transfers between devices: 0.37 us -> 17.8 us
    all_gather x7 -> x0, blocking collectives: 93.3 us -> none  [settle(): lax.all_gather(summed.astype(jnp.bfloat16), 'row', axis=2, tiled=True)]
    all_to_all x0 -> x5, blocking collectives: none -> 57.2 us  [settle(): lax.all_to_all(jnp.stack([summed.astype(jnp.bfloat16)] * lax.axis_size('r...]
    all_gather x2 -> x0, waiting for transfers between devices: 40 us -> none  [settle(): lax.all_gather(summed.astype(jnp.bfloat16), 'row', axis=2, tiled=True)]
    all_to_all x0 -> x4, waiting for transfers between devices: none -> 22.3 us  [settle(): lax.all_to_all(jnp.stack([summed.astype(jnp.bfloat16)] * lax.axis_size('r...]
    all_to_all x0 -> x4, starting transfers between devices: none -> 17.7 us  [settle(): lax.all_to_all(jnp.stack([summed.astype(jnp.bfloat16)] * lax.axis_size('r...]
  transfers between devices with their start and end apart: 9 -> 11, of which waited for: 9 -> 11; matrix products, arithmetic and copies ran while one was open for 2% -> 2% of each run, Pallas kernels for 0% -> 0%
where the time goes in v1:
time: 1040 us
  waiting for transfers between devices  516 us (50%)
  blocking collectives  434 us (42%)
  local copies, waits for them, and re-layouts  39.2 us (4%)
  starting transfers between devices  17.8 us (2%)
  between operations  14.6 us (1%)
    psum x5, waiting for transfers between devices, settle(): summed = lax.psum(partial_value, 'col')  402 us
    psum x5, blocking collectives, settle(): summed = lax.psum(partial_value, 'col')  377 us
    all_gather x1, waiting for transfers between devices, per_device(): lax.all_gather(rhs_half[0, 1:3].astype(jnp.bfloat16), ('row', 'col'), axi...  70.4 us
    all_to_all x5, blocking collectives, settle(): lax.all_to_all(jnp.stack([summed.astype(jnp.bfloat16)] * lax.axis_size('r...  57.2 us
    all_to_all x4, waiting for transfers between devices, settle(): lax.all_to_all(jnp.stack([summed.astype(jnp.bfloat16)] * lax.axis_size('r...  22.3 us
    psum x1, waiting for transfers between devices, per_device(): root_terms = lax.psum(root_terms, 'gz')  21.4 us
  transfers between devices with their start and end apart: 11, of which 11 were waited for; matrix products, arithmetic and copies ran while one was open for 2% of the time, Pallas kernels for 0%

profile of v1, /device:TPU:0, one launch (start us, length us, event | category | flops | bytes accessed | tf_op | source)
XLA Modules:
  0.0 1041.0 jit_solution(16283220339171751882)
XLA Ops:
  8.9 70.4 %all-gather.3.cloned.1.call-done = bf16[1,2,64,4096]{2,1,0,3:T(2,128)(2,1)} async-done(((bf16[1,2,64,64]{2,1,0,3:T(2,128)(2,1)}), bf16[1,2,64,4096]{2,1,0,3:T(2,128)(2,1)}) %all-gather.3.cloned.1.call-update) | async-done | bytes 1048592 | tf_op jit(solution)/shard_map/all_gather | solution.py:61
  83.3 83.1 %all-reduce.12.cloned.1.call-done = f32[2,64,1024]{2,1,0:T(8,128)} async-done(((f32[2,64,1024]{2,1,0:T(8,128)}), f32[2,64,1024]{2,1,0:T(8,128)}) %all-reduce.12.cloned.1.call-update) | async-done | bytes 524304 | tf_op jit(solution)/shard_map/psum | solution.py:28
  168.7 4.4 all-to-all-start
  177.4 9.0 all-to-all-done
  189.5 75.3 %all-reduce.23 = bf16[1,64,1024]{2,1,0:T(8,128)(2,1)} all-reduce(f32[1,64,1024]{2,1,0:T(8,128)S(1)} %dynamic_update_slice.31), channel_id=1, replica_groups=mesh['row'=4,'col'=16,'gz'=2] {'col'}, use_global_device_ids=true, to_apply=%region_1.0 | all-reduce | flops 65536 | bytes 393216 | tf_op jit(solution)/shard_map/psum | solution.py:28
  265.8 10.5 %all_to_all.45 = bf16[4,1,64,1024]{3,2,1,0:T(8,128)(2,1)S(1)} all-to-all(bf16[4,1,64,1024]{3,2,1,0:T(8,128)(2,1)S(1)} %stack.19), channel_id=1, replica_groups=mesh['row'=4,'col'=16,'gz'=2] {'row'}, dimensions={0} | all-to-all | bytes 1048576 | tf_op jit(solution)/shard_map/all_to_all | solution.py:31
  278.8 80.0 %all-reduce.14.cloned.1.call-done = f32[1,64,1024]{2,1,0:T(8,128)} async-done(((f32[1,64,1024]{2,1,0:T(8,128)}), f32[1,64,1024]{2,1,0:T(8,128)}) %all-reduce.14.cloned.1.call-update) | async-done | bytes 262160 | tf_op jit(solution)/shard_map/psum | solution.py:28
  360.6 4.4 all-to-all-start.2
  368.9 4.3 all-to-all-done.2
  375.5 21.4 %all-reduce.16.cloned.1.call-done = f32[1,64,1024]{2,1,0:T(8,128)} async-done(((f32[1,64,1024]{2,1,0:T(8,128)}), f32[1,64,1024]{2,1,0:T(8,128)}) %all-reduce.16.cloned.1.call-update) | async-done | bytes 262160 | tf_op jit(solution)/shard_map/psum | solution.py:75
  399.2 77.5 %all-reduce.24 = bf16[1,64,1024]{2,1,0:T(8,128)(2,1)S(1)} all-reduce(f32[1,64,1024]{2,1,0:T(8,128)} %dynamic_update_slice.33), channel_id=1, replica_groups=mesh['row'=4,'col'=16,'gz'=2] {'col'}, use_global_device_ids=true, to_apply=%region_4.0 | all-reduce | flops 65536 | bytes 393216 | tf_op jit(solution)/shard_map/psum | solution.py:28
  476.8 12.3 %all_to_all.46 = bf16[4,1,64,1024]{3,2,1,0:T(8,128)(2,1)S(1)} all-to-all(bf16[4,1,64,1024]{3,2,1,0:T(8,128)(2,1)S(1)} %stack.21), channel_id=1, replica_groups=mesh['row'=4,'col'=16,'gz'=2] {'row'}, dimensions={0} | all-to-all | bytes 1048576 | tf_op jit(solution)/shard_map/all_to_all | solution.py:31
  489.8 71.8 %all-reduce.25 = bf16[1,64,1024]{2,1,0:T(8,128)(2,1)S(1)} all-reduce(f32[1,64,1024]{2,1,0:T(8,128)S(1)} %dynamic_update_slice.34), channel_id=1, replica_groups=mesh['row'=4,'col'=16,'gz'=2] {'col'}, use_global_device_ids=true, to_apply=%region_5.0 | all-reduce | flops 65536 | bytes 393216 | tf_op jit(solution)/shard_map/psum | solution.py:28
  561.7 10.5 %all_to_all.47 = bf16[4,1,64,1024]{3,2,1,0:T(8,128)(2,1)S(1)} all-to-all(bf16[4,1,64,1024]{3,2,1,0:T(8,128)(2,1)S(1)} %stack.22), channel_id=1, replica_groups=mesh['row'=4,'col'=16,'gz'=2] {'row'}, dimensions={0} | all-to-all | bytes 1048576 | tf_op jit(solution)/shard_map/all_to_all | solution.py:31
  574.9 80.6 %all-reduce.18.cloned.1.call-done = f32[1,64,1024]{2,1,0:T(8,128)} async-done(((f32[1,64,1024]{2,1,0:T(8,128)}), f32[1,64,1024]{2,1,0:T(8,128)}) %all-reduce.18.cloned.1.call-update) | async-done | bytes 262160 | tf_op jit(solution)/shard_map/psum | solution.py:28
  657.4 4.4 all-to-all-start.5
  663.5 6.4 all-to-all-done.5
  673.8 74.5 %all-reduce.26 = bf16[1,64,1024]{2,1,0:T(8,128)(2,1)S(1)} all-reduce(f32[1,64,1024]{2,1,0:T(8,128)S(1)} %dynamic_update_slice.36), channel_id=1, replica_groups=mesh['row'=4,'col'=16,'gz'=2] {'col'}, use_global_device_ids=true, to_apply=%region_7.0 | all-reduce | flops 65536 | bytes 393216 | tf_op jit(solution)/shard_map/psum | solution.py:28
  748.4 10.5 %all_to_all.48 = bf16[4,1,64,1024]{3,2,1,0:T(8,128)(2,1)S(1)} all-to-all(bf16[4,1,64,1024]{3,2,1,0:T(8,128)(2,1)S(1)} %stack.24), channel_id=1, replica_groups=mesh['row'=4,'col'=16,'gz'=2] {'row'}, dimensions={0} | all-to-all | bytes 1048576 | tf_op jit(solution)/shard_map/all_to_all | solution.py:31
  761.4 80.0 %all-reduce.20.cloned.1.call-done = f32[1,64,1024]{2,1,0:T(8,128)} async-done(((f32[1,64,1024]{2,1,0:T(8,128)}), f32[1,64,1024]{2,1,0:T(8,128)}) %all-reduce.20.cloned.1.call-update) | async-done | bytes 262160 | tf_op jit(solution)/shard_map/psum | solution.py:28
  843.2 4.4 all-to-all-start.7
  858.6 77.8 %all-reduce.27 = bf16[2,64,1024]{2,1,0:T(8,128)(2,1)S(1)} all-reduce(f32[2,64,1024]{2,1,0:T(8,128)S(1)} %dynamic_update_slice.38), channel_id=1, replica_groups=mesh['row'=4,'col'=16,'gz'=2] {'col'}, use_global_device_ids=true, to_apply=%region_9.0 | all-reduce | flops 131072 | bytes 786432 | tf_op jit(solution)/shard_map/psum | solution.py:28
  936.6 13.4 %all_to_all.49 = bf16[4,2,64,1024]{3,2,1,0:T(8,128)(2,1)S(1)} all-to-all(bf16[4,2,64,1024]{3,2,1,0:T(8,128)(2,1)S(1)} %stack.26), channel_id=1, replica_groups=mesh['row'=4,'col'=16,'gz'=2] {'row'}, dimensions={0} | all-to-all | bytes 2097152 | tf_op jit(solution)/shard_map/all_to_all | solution.py:31
  954.1 78.5 %all-reduce.22.cloned.1.call-done = f32[2,64,1024]{2,1,0:T(8,128)} async-done(((f32[2,64,1024]{2,1,0:T(8,128)}), f32[2,64,1024]{2,1,0:T(8,128)}) %all-reduce.22.cloned.1.call-update) | async-done | bytes 524304 | tf_op jit(solution)/shard_map/psum | solution.py:28
  (120 shorter events, 60.7 us)
Async XLA Ops:
  7.2 481.9 %copy-start = (bf16[256,1024]{1,0:T(8,128)(2,1)S(1)}, bf16[256,1024]{1,0:T(8,128)(2,1)}, u32[]{:S(2)}) copy-start(bf16[256,1024]{1,0:T(8,128)(2,1)} %param.18) | copy-start | bytes 1572868
  7.2 72.2 %all-gather.3.cloned.1.call-start = ((), (), s32[]{:S(2)}) async-start(), calls=%async_computation.15 | async-start | bytes 2129920 | tf_op jit(solution)/shard_map/all_gather | solution.py:61
  8.9 157.6 %all-reduce.12.cloned.1.call-start = ((), (), s32[]{:S(2)}) async-start(), calls=%async_computation.9 | async-start | bytes 1048576 | tf_op jit(solution)/shard_map/psum | solution.py:28
  82.5 0.8 copy-start.4
  83.3 89.8 %copy-start.2 = (bf16[1,5,256,1024]{3,2,1,0:T(8,128)(2,1)S(1)}, bf16[1,5,256,1024]{3,2,1,0:T(8,128)(2,1)}, u32[]{:S(2)}) copy-start(bf16[1,5,256,1024]{3,2,1,0:T(8,128)(2,1)} %param.12) | copy-start | bytes 7864324
  168.7 17.7 %all-to-all-start = ((bf16[4,2,64,1024]{3,2,1,0:T(8,128)(2,1)}), bf16[4,2,64,1024]{3,2,1,0:T(8,128)(2,1)}, u32[]{:S(2)}, u32[]{:S(2)}) async-start(bf16[4,2,64,1024]{3,2,1,0:T(8,128)(2,1)} %stack.18), calls=%async_computation | async-start | bytes 2097152 | tf_op jit(solution)/shard_map/all_to_all | solution.py:31
  173.1 185.7 %all-reduce.14.cloned.1.call-start = ((), (), s32[]{:S(2)}) async-start(), calls=%async_computation.10 | async-start | bytes 524288 | tf_op jit(solution)/shard_map/psum | solution.py:28
  186.4 1.5 copy-start.1
  278.1 0.7 copy-start.7
  360.6 12.6 %all-to-all-start.2 = ((bf16[4,1,64,1024]{3,2,1,0:T(8,128)(2,1)}), bf16[4,1,64,1024]{3,2,1,0:T(8,128)(2,1)}, u32[]{:S(2)}, u32[]{:S(2)}) async-start(bf16[4,1,64,1024]{3,2,1,0:T(8,128)(2,1)} %stack.20), calls=%async_computation.2 | async-start | bytes 1048576 | tf_op jit(solution)/shard_map/all_to_all | solution.py:31
  365.1 31.9 %all-reduce.16.cloned.1.call-start = ((), (), s32[]{:S(2)}) async-start(), calls=%async_computation.11 | async-start | bytes 524288 | tf_op jit(solution)/shard_map/psum | solution.py:75
  368.9 28.0 %copy-start.11 = (f32[64,64]{1,0:T(8,128)S(1)}, f32[64,64]{1,0:T(8,128)}, u32[]{:S(2)}) copy-start(f32[64,64]{1,0:T(8,128)} %param.11) | copy-start | bytes 49156
  375.5 280.1 %all-reduce.18.cloned.1.call-start = ((), (), s32[]{:S(2)}) async-start(), calls=%async_computation.12 | async-start | bytes 524288 | tf_op jit(solution)/shard_map/psum | solution.py:28
  572.2 89.6 %copy-start.13 = (s32[1,5,2,8]{3,2,1,0:T(2,128)S(1)}, s32[1,5,2,8]{3,2,1,0:T(2,128)}, u32[]{:S(2)}) copy-start(s32[1,5,2,8]{3,2,1,0:T(2,128)} %param.15) | copy-start | bytes 964
  572.2 89.6 %copy-start.3 = (bf16[1,5,256,1024]{3,2,1,0:T(8,128)(2,1)S(1)}, bf16[1,5,256,1024]{3,2,1,0:T(8,128)(2,1)}, u32[]{:S(2)}) copy-start(bf16[1,5,256,1024]{3,2,1,0:T(8,128)(2,1)} %param.14) | copy-start | bytes 7864324
  574.2 0.7 copy-start.8
  657.4 12.6 %all-to-all-start.5 = ((bf16[4,1,64,1024]{3,2,1,0:T(8,128)(2,1)}), bf16[4,1,64,1024]{3,2,1,0:T(8,128)(2,1)}, u32[]{:S(2)}, u32[]{:S(2)}) async-start(bf16[4,1,64,1024]{3,2,1,0:T(8,128)(2,1)} %stack.23), calls=%async_computation.5 | async-start | bytes 1048576 | tf_op jit(solution)/shard_map/all_to_all | solution.py:31
  661.8 179.6 %all-reduce.20.cloned.1.call-start = ((), (), s32[]{:S(2)}) async-start(), calls=%async_computation.13 | async-start | bytes 524288 | tf_op jit(solution)/shard_map/psum | solution.py:28
  671.0 2.3 copy-start.10
  760.7 0.7 copy-start.9
  843.2 12.6 %all-to-all-start.7 = ((bf16[4,1,64,1024]{3,2,1,0:T(8,128)(2,1)}), bf16[4,1,64,1024]{3,2,1,0:T(8,128)(2,1)}, u32[]{:S(2)}, u32[]{:S(2)}) async-start(bf16[4,1,64,1024]{3,2,1,0:T(8,128)(2,1)} %stack.25), calls=%async_computation.7 | async-start | bytes 1048576 | tf_op jit(solution)/shard_map/all_to_all | solution.py:31
  847.6 185.0 %all-reduce.22.cloned.1.call-start = ((), (), s32[]{:S(2)}) async-start(), calls=%async_computation.14 | async-start | bytes 1048576 | tf_op jit(solution)/shard_map/psum | solution.py:28
  936.6 13.6 %copy-start.6 = (bf16[1,3,256,1024]{3,2,1,0:T(8,128)(2,1)S(1)}, bf16[1,3,256,1024]{3,2,1,0:T(8,128)(2,1)}, u32[]{:S(2)}) copy-start(bf16[1,3,256,1024]{3,2,1,0:T(8,128)(2,1)} %param.17) | copy-start | bytes 4718596
  951.0 0.8 copy-start.5
  (1 other events, 0.7 us)
Sparse Core Ops, SparseCore 0:
  11.4 67.8 all-gather.2
  83.4 82.9 all-reduce.11
  278.9 79.8 all-reduce.13
  375.6 21.2 all-reduce.15
  575.0 80.4 all-reduce.17
  761.5 79.7 all-reduce.19
  952.0 80.5 all-reduce.21
